TPU v7x, 512 devices: a whole 4x4x16 slice. The times are simulated.
512 devices in a mesh: ctx: 32 (over z, core), ch: 16 (over x, y).
Axes of the slice: x: 4, y: 4, z: 16, core: 2. Of those that a mesh axis runs over, the one named last changes fastest.
Arguments:
- query_in: bfloat16 [8192, 4096], P('ctx', 'ch'), may hold values from -63 to 63
- key_in: bfloat16 [8192, 4096], P('ctx', 'ch'), may hold values from -4 to 4
- value_in: bfloat16 [8192, 4096], P('ctx', 'ch'), may hold values from -4 to 4
- short_taps: float32 [7, 3, 4096], P(None, None, 'ch'), may hold values from -2 to 2
- residues: float32 [4096, 16], P('ch'), may hold values from -1.5 to 1.5
- decays: float32 [4096, 16], P('ch'), may hold values from 6.1035157e-06 to 0.02
- out_weight: bfloat16 [4096, 4096], P('ch'), may hold values from -0.125 to 0.125
- out_grad: bfloat16 [8192, 4096], P('ctx', 'ch'), may hold values from -6 to 6
Outputs:
- projected: bfloat16 [8192, 4096], P('ctx', 'ch')
- grad_query: bfloat16 [8192, 4096], P('ctx', 'ch')
- grad_key: bfloat16 [8192, 4096], P('ctx', 'ch')
- grad_value: bfloat16 [8192, 4096], P('ctx', 'ch')
All inputs are finite; a program needn't handle non-finite values.
Results may differ from a plain program's by a relative error of at most 0.0058.
Values may be sent and summed in bfloat16 or wider, within the bound.
A program may use at most 64 MiB of HBM per device.

v0:
```python
import jax
import jax.numpy as jnp
import numpy as np
from jax import lax
from jax.sharding import PartitionSpec as P

block_len = 64
exact_precision = lax.Precision.HIGHEST


def from_behind(value, axis, steps):
    count = lax.axis_size(axis)
    leading, last = (max(0, -steps), min(count, count - steps))
    return lax.ppermute(value, axis, [(source, source + steps) for source in range(leading, last)])


def one_hot_table():
    indices = np.arange(block_len)
    return (indices[None, :, None] - indices[None, None, :] == indices[:, None, None]).astype(
        np.float32
    )


def modal_tables(residues, decays):
    offsets = jnp.arange(block_len, dtype=jnp.float32)
    scaled = residues * jnp.sqrt(decays)
    filter_head = jnp.einsum(
        "cn,cnd->cd", scaled, jnp.exp(-decays[:, :, None] * offsets), precision=exact_precision
    )
    toeplitz = jnp.einsum(
        "cd,dij->cij", filter_head, jnp.asarray(one_hot_table()), precision=exact_precision
    )
    decay_in = jnp.exp(-decays[:, :, None] * (block_len - 1.0 - offsets))
    decay_out = scaled[:, :, None] * jnp.exp(-decays[:, :, None] * (offsets + 1.0))
    return (toeplitz, decay_in, decay_out)


def combine(earlier, latter):
    return (earlier[0] * latter[1] + latter[0], earlier[1] * latter[1])


def prepare(signal, decays, decay_tables):
    channels, length = signal.shape
    pieces = length // block_len
    block_list = signal.reshape(channels, pieces, block_len)
    within_block = jnp.einsum(
        "cij,cbj->cbi", decay_tables[0], block_list, precision=exact_precision
    )
    block_final_states = jnp.einsum(
        "avp,axp->avx", block_list, decay_tables[1], precision=exact_precision
    )
    factor = jnp.broadcast_to(jnp.exp(-decays * block_len)[:, None, :], block_final_states.shape)
    running, _ = lax.associative_scan(combine, (block_final_states, factor), axis=1)
    return (within_block, running)


def finish(within_block, running, decays, incoming, decay_tables):
    channels, pieces, _ = within_block.shape
    earlier_sum = jnp.concatenate([jnp.zeros_like(running[:, :1]), running[:, :-1]], axis=1)
    starts = jnp.arange(pieces, dtype=jnp.float32) * block_len
    carried_state = (
        earlier_sum + jnp.exp(-decays[:, None, :] * starts[None, :, None]) * incoming[:, None, :]
    )
    final_output = within_block + jnp.einsum(
        "lpe,leo->lpo", carried_state, decay_tables[2], precision=exact_precision
    )
    return final_output.reshape(channels, pieces * block_len)


def channel_params(residues, decays):
    part_size = residues.shape[0] // lax.axis_size("ctx")
    first_chan = lax.axis_index("ctx") * part_size
    residues = lax.dynamic_slice_in_dim(residues, first_chan, part_size, 0)
    decays = lax.dynamic_slice_in_dim(decays, first_chan, part_size, 0)
    return (decays, modal_tables(residues, decays))


def long_forward(mixed_values, decays, decay_tables):
    sequence = lax.all_to_all(mixed_values.T, "ctx", split_axis=0, concat_axis=1, tiled=True)
    within_block, running = prepare(sequence.astype(jnp.float32), decays, decay_tables)
    final_output = finish(
        within_block, running, decays, jnp.zeros(decays.shape, jnp.float32), decay_tables
    )
    return lax.all_to_all(final_output, "ctx", split_axis=1, concat_axis=0, tiled=True).T


def long_backward(grad_mixed, decays, decay_tables):
    sequence = lax.all_to_all(grad_mixed.T, "ctx", split_axis=0, concat_axis=1, tiled=True)
    within_block, running = prepare(jnp.flip(sequence.astype(jnp.float32), 1), decays, decay_tables)
    final_output = jnp.flip(
        finish(within_block, running, decays, jnp.zeros(decays.shape, jnp.float32), decay_tables), 1
    )
    return lax.all_to_all(final_output, "ctx", split_axis=1, concat_axis=0, tiled=True).T


def shards(query_in, key_in, value_in, short_taps, residues, decays, out_weight, out_grad):
    length = query_in.shape[0]
    rim_len = short_taps.shape[0] - 1
    stacked = jnp.stack([query_in, key_in, value_in])
    ahead_rows = from_behind(stacked[:, length - rim_len :], "ctx", 1)
    extended = jnp.concatenate([ahead_rows, stacked], axis=1).astype(jnp.float32)
    featured = jnp.zeros(stacked.shape, jnp.float32)
    for tap_index in range(rim_len + 1):
        begin = rim_len - tap_index
        featured = (
            featured + short_taps[tap_index][:, None, :] * extended[:, begin : begin + length]
        )
    query_feat = featured[0]
    key_feat = featured[1]
    value_feat = featured[2]
    mixed_values = (key_feat * value_feat).astype(jnp.bfloat16)
    used_decays, decay_tables = channel_params(residues, decays)
    conv_out = long_forward(mixed_values, used_decays, decay_tables)
    gated = (query_feat * conv_out).astype(jnp.bfloat16)
    partial_proj = jnp.dot(gated, out_weight, preferred_element_type=jnp.float32)
    projected = lax.psum_scatter(partial_proj, "ch", scatter_dimension=1, tiled=True).astype(
        jnp.bfloat16
    )
    grad_gated = jnp.einsum(
        "te,ce->tc",
        lax.all_gather(out_grad, "ch", axis=1, tiled=True),
        out_weight,
        preferred_element_type=jnp.float32,
    )
    grad_query_feat = (grad_gated * conv_out).astype(jnp.bfloat16)
    grad_mixed = (grad_gated * query_feat).astype(jnp.bfloat16)
    grad_conv = long_backward(grad_mixed, used_decays, decay_tables)
    grad_key_feat = (grad_conv * value_feat).astype(jnp.bfloat16)
    grad_value_feat = (grad_conv * key_feat).astype(jnp.bfloat16)
    grad_feats = jnp.stack([grad_query_feat, grad_key_feat, grad_value_feat])
    behind = from_behind(grad_feats[:, :rim_len], "ctx", -1)
    widened = jnp.concatenate([grad_feats, behind], axis=1).astype(jnp.float32)
    grad_stack = jnp.zeros(grad_feats.shape, jnp.float32)
    for tap_index in range(rim_len + 1):
        grad_stack = (
            grad_stack
            + short_taps[tap_index][:, None, :] * widened[:, tap_index : tap_index + length]
        )
    grad_stack = grad_stack.astype(jnp.bfloat16)
    return (projected, grad_stack[0], grad_stack[1], grad_stack[2])


def solution(mesh):
    in_specs = (
        P("ctx", "ch"),
        P("ctx", "ch"),
        P("ctx", "ch"),
        P(None, None, "ch"),
        P("ch", None),
        P("ch", None),
        P("ch", None),
        P("ctx", "ch"),
    )
    out_specs = (P("ctx", "ch"), P("ctx", "ch"), P("ctx", "ch"), P("ctx", "ch"))
    return jax.shard_map(shards, mesh=mesh, in_specs=in_specs, out_specs=out_specs, check_vma=False)
```

profile of v0, /device:TPU:1, one launch (start us, length us, event | category | flops | bytes accessed | tf_op | source)
XLA Modules:
  0.0 458.4 jit_solution(5360661742519281431)
XLA Ops:
  8.6 4.9 %collective-permute-start = (bf16[3,6,256]{2,1,0:T(8,128)(2,1)S(1)}, bf16[3,6,256]{2,1,0:T(8,128)(2,1)S(1)}, u32[]{:S(2)}, u32[]{:S(2)}) collective-permute-start(bf16[3,6,256]{2,1,0:T(8,128)(2,1)S(1)} %pad_maximum_fusion.14), channel_id=1, source_target_pairs={{0,16},{16,32},{32,48},{48,64},{64,80},{80,96},{96,112},{112,128},... | collective-permute-start | bytes 27656 | tf_op jit(solution)/shard_map/ppermute | solution.py:14
  21.3 56.0 %all-gather.2.cloned.1.call-done = bf16[256,4096]{1,0:T(8,128)(2,1)} async-done(((bf16[256,256]{1,0:T(8,128)(2,1)}), bf16[256,4096]{1,0:T(8,128)(2,1)}) %all-gather.2.cloned.1.call-update) | async-done | bytes 2097168 | tf_op jit(solution)/shard_map/all_gather | solution.py:121
  77.3 2.3 fusion.74
  80.4 14.4 %all-to-all-start.2 = ((bf16[32,8,256]{2,1,0:T(8,128)(2,1)}), bf16[32,8,256]{2,1,0:T(8,128)(2,1)S(1)}, u32[]{:S(2)}, u32[]{:S(2)}) async-start(bf16[32,8,256]{2,1,0:T(8,128)(2,1)} %bitcast.21), calls=%async_computation.3 | async-start | bytes 262144 | tf_op jit(solution)/shard_map/all_to_all | solution.py:88
  95.3 3.4 fusion.73
  98.7 12.0 %all-to-all-done.2 = bf16[32,8,256]{2,1,0:T(8,128)(2,1)S(1)} async-done(((bf16[32,8,256]{2,1,0:T(8,128)(2,1)}), bf16[32,8,256]{2,1,0:T(8,128)(2,1)S(1)}, u32[]{:S(2)}, u32[]{:S(2)}) %all-to-all-start.2) | async-done | bytes 131104 | tf_op jit(solution)/shard_map/all_to_all | solution.py:88
  110.7 21.2 %rev.7 = f32[8,8192]{1,0:T(8,128)} reverse(f32[8,8192]{1,0:T(8,128)S(1)} %bitcast.137), dimensions={1} | reverse | bytes 524288 | tf_op jit(solution)/shard_map/jit(_flip)/rev | solution.py:89
  134.6 1.8 slice.453
  137.5 1.8 slice.423
  149.3 1.6 slice.447
  150.9 1.7 slice.433
  152.6 1.7 slice.432
  162.9 2.8 fusion.17
  172.2 3.2 pad.107
  177.7 3.2 pad.109
  191.1 2.1 convolution_add_fusion
  195.2 24.0 %rev.8 = f32[8,8192]{1,0:T(8,128)S(1)} reverse(f32[8,8192]{1,0:T(8,128)} %reshape.69), dimensions={1} | reverse | bytes 524288 | tf_op jit(solution)/shard_map/jit(_flip)/rev | solution.py:90
  219.2 26.5 %all_to_all.67 = f32[8,32,256]{2,0,1:T(8,128)} all-to-all(f32[8,32,256]{2,0,1:T(8,128)S(1)} %bitcast.138), channel_id=1, replica_groups=mesh['ctx'=32,'ch'=16] {'ctx'}, dimensions={1} | all-to-all | bytes 524288 | tf_op jit(solution)/shard_map/all_to_all | solution.py:93
  248.6 20.0 %all_to_all.68 = bf16[32,8,256]{2,1,0:T(8,128)(2,1)S(1)} all-to-all(bf16[32,8,256]{2,1,0:T(8,128)(2,1)S(1)} %bitcast.147), channel_id=1, replica_groups=mesh['ctx'=32,'ch'=16] {'ctx'}, dimensions={0} | all-to-all | bytes 262144 | tf_op jit(solution)/shard_map/all_to_all | solution.py:79
  272.8 1.8 slice.420
  288.5 3.1 pad.91
  295.4 4.9 %pad.92 = f32[8,8,16]{1,2,0:T(8,128)} pad(f32[8,4,16]{1,2,0:T(8,128)} %pad_maximum_fusion.1, f32[]{:T(128)} %constant.7.clone.1), padding=0_0_0x0_1_1x0_0_0 | pad | bytes 6148 | tf_op jit(solution)/shard_map/pad | solution.py:53
  300.3 4.9 %pad.93 = f32[8,8,16]{1,2,0:T(8,128)} pad(f32[8,4,16]{1,2,0:T(8,128)} %add.260, f32[]{:T(128)} %constant.7.clone.1), padding=0_0_0x1_0_1x0_0_0 | pad | bytes 6148 | tf_op jit(solution)/shard_map/pad | solution.py:53
  308.5 3.2 pad.94
  311.7 5.0 %pad.95 = f32[8,16,16]{1,2,0:T(8,128)} pad(f32[8,8,16]{1,2,0:T(8,128)} %add.262, f32[]{:T(128)} %constant.7.clone.1), padding=0_0_0x1_0_1x0_0_0 | pad | bytes 12292 | tf_op jit(solution)/shard_map/pad | solution.py:53
  320.0 3.3 pad.97
  326.0 3.5 pad.99
  333.8 2.1 convolution_add_fusion.1
  339.0 25.9 %all_to_all.69 = f32[8,32,256]{2,0,1:T(8,128)S(1)} all-to-all(f32[8,32,256]{2,0,1:T(8,128)S(1)} %copy.85), channel_id=1, replica_groups=mesh['ctx'=32,'ch'=16] {'ctx'}, dimensions={1} | all-to-all | bytes 524288 | tf_op jit(solution)/shard_map/all_to_all | solution.py:84
  365.1 2.7 fusion.24
  368.8 3.4 collective-permute-start.1
  375.4 74.6 %reduce-scatter.2.cloned.1.call-done = f32[256,256]{1,0:T(8,128)} async-done(((f32[256,4096]{1,0:T(8,128)}), f32[256,256]{1,0:T(8,128)}) %reduce-scatter.2.cloned.1.call-update) | async-done | bytes 262160 | tf_op jit(solution)/shard_map/reduce_scatter | solution.py:116
  (203 shorter events, 100.7 us)
Async XLA Ops:
  7.2 70.1 %copy-start = (bf16[256,4096]{1,0:T(8,128)(2,1)S(1)}, bf16[256,4096]{1,0:T(8,128)(2,1)}, u32[]{:S(2)}) copy-start(bf16[256,4096]{1,0:T(8,128)(2,1)} %param.15) | copy-start | bytes 6291460
  7.2 70.1 %all-gather.2.cloned.1.call-start = ((), (), s32[]{:S(2)}) async-start(), calls=%async_computation.6 | async-start | bytes 2228224 | tf_op jit(solution)/shard_map/all_gather | solution.py:121
  8.6 10.8 %collective-permute-start = (bf16[3,6,256]{2,1,0:T(8,128)(2,1)S(1)}, bf16[3,6,256]{2,1,0:T(8,128)(2,1)S(1)}, u32[]{:S(2)}, u32[]{:S(2)}) collective-permute-start(bf16[3,6,256]{2,1,0:T(8,128)(2,1)S(1)} %pad_maximum_fusion.14), channel_id=1, source_target_pairs={{0,16},{16,32},{32,48},{48,64},{64,80},{80,96},{96,112},{112,128},... | collective-permute-start | bytes 27656 | tf_op jit(solution)/shard_map/ppermute | solution.py:14
  16.6 4.6 copy-start.16
  16.6 4.6 copy-start.18
  16.7 4.5 copy-start.20
  16.7 4.5 copy-start.22
  16.7 4.5 copy-start.24
  16.7 4.5 copy-start.26
  17.3 77.7 %copy-start.14 = (f32[8,16]{1,0:T(8,128)}, f32[8,16]{1,0:T(8,128)S(1)}, u32[]{:S(2)}) copy-start(f32[8,16]{1,0:T(8,128)S(1)} %get-tuple-element.34) | copy-start | bytes 1540
  79.6 31.1 %copy-start.1 = (f32[256,256]{1,0:T(8,128)}, f32[256,256]{1,0:T(8,128)S(1)}, u32[]{:S(2)}) copy-start(f32[256,256]{1,0:T(8,128)S(1)} %fusion.74) | copy-start | bytes 786436
  80.4 30.2 %all-to-all-start.2 = ((bf16[32,8,256]{2,1,0:T(8,128)(2,1)}), bf16[32,8,256]{2,1,0:T(8,128)(2,1)S(1)}, u32[]{:S(2)}, u32[]{:S(2)}) async-start(bf16[32,8,256]{2,1,0:T(8,128)(2,1)} %bitcast.21), calls=%async_computation.3 | async-start | bytes 262144 | tf_op jit(solution)/shard_map/all_to_all | solution.py:88
  94.8 355.2 %reduce-scatter.2.cloned.1.call-start = ((), (), s32[]{:S(2)}) async-start(), calls=%async_computation.5 | async-start | bytes 4456448 | tf_op jit(solution)/shard_map/reduce_scatter | solution.py:116
  134.6 4.7 %copy-start.8 = (f32[8,128,16]{1,2,0:T(8,128)}, f32[8,128,16]{1,2,0:T(8,128)S(1)}, u32[]{:S(2)}) copy-start(f32[8,128,16]{1,2,0:T(8,128)S(1)} %fusion.42) | copy-start | bytes 196612
  144.8 15.8 %copy-start.4 = (f32[8,32,16]{1,2,0:T(8,128)}, f32[8,32,16]{1,2,0:T(8,128)S(1)}, u32[]{:S(2)}) copy-start(f32[8,32,16]{1,2,0:T(8,128)S(1)} %multiply_add_fusion.4) | copy-start | bytes 49156
  165.7 5.8 %copy-start.7 = (f32[8,8,16]{1,2,0:T(8,128)S(1)}, f32[8,8,16]{1,2,0:T(8,128)}, u32[]{:S(2)}) copy-start(f32[8,8,16]{1,2,0:T(8,128)} %multiply_add_fusion.2) | copy-start | bytes 12292
  165.7 11.2 %copy-start.6 = (f32[8,16,16]{1,2,0:T(8,128)S(1)}, f32[8,16,16]{1,2,0:T(8,128)}, u32[]{:S(2)}) copy-start(f32[8,16,16]{1,2,0:T(8,128)} %multiply_add_fusion.3) | copy-start | bytes 24580
  165.7 16.2 %copy-start.5 = (f32[8,32,16]{1,2,0:T(8,128)S(1)}, f32[8,32,16]{1,2,0:T(8,128)}, u32[]{:S(2)}) copy-start(f32[8,32,16]{1,2,0:T(8,128)} %copy-done.4) | copy-start | bytes 49156
  169.9 17.8 %copy-start.9 = (f32[8,128,16]{1,2,0:T(8,128)S(1)}, f32[8,128,16]{1,2,0:T(8,128)}, u32[]{:S(2)}) copy-start(f32[8,128,16]{1,2,0:T(8,128)} %copy-done.8) | copy-start | bytes 196612
  171.6 19.5 %copy-start.12 = (f32[8,128,64]{1,2,0:T(8,128)S(1)}, f32[8,128,64]{1,2,0:T(8,128)}, u32[]{:S(2)}) copy-start(f32[8,128,64]{1,2,0:T(8,128)} %fusion.17) | copy-start | bytes 786436
  195.2 75.1 %copy-start.3 = (f32[8,64,64]{2,0,1:T(8,128)S(1)}, f32[8,64,64]{2,0,1:T(8,128)}, u32[]{:S(2)}) copy-start(f32[8,64,64]{2,0,1:T(8,128)} %fusion.73) | copy-start | bytes 393220
  272.8 9.6 %copy-start.13 = (f32[8,16]{1,0:T(8,128)S(1)}, f32[8,16]{1,0:T(8,128)}, u32[]{:S(2)}) copy-start(f32[8,16]{1,0:T(8,128)} %get-tuple-element.30) | copy-start | bytes 1540
  295.4 38.3 %copy-start.11 = (f32[8,128,64]{1,2,0:T(8,128)S(1)}, f32[8,128,64]{1,2,0:T(8,128)}, u32[]{:S(2)}) copy-start(f32[8,128,64]{1,2,0:T(8,128)} %fusion.19) | copy-start | bytes 786436
  319.1 14.7 %copy-start.15 = (f32[8,16]{1,0:T(8,128)S(1)}, f32[8,16]{1,0:T(8,128)}, u32[]{:S(2)}) copy-start(f32[8,16]{1,0:T(8,128)} %copy-done.14) | copy-start | bytes 1540
  368.7 5.2 %copy-start.17 = (f32[3,256]{1,0:T(4,128)S(1)}, f32[3,256]{1,0:T(4,128)}, u32[]{:S(2)}) copy-start(f32[3,256]{1,0:T(4,128)} %copy-done.16) | copy-start | bytes 9220
  368.7 5.2 %copy-start.19 = (f32[3,256]{1,0:T(4,128)S(1)}, f32[3,256]{1,0:T(4,128)}, u32[]{:S(2)}) copy-start(f32[3,256]{1,0:T(4,128)} %copy-done.18) | copy-start | bytes 9220
  368.7 5.2 %copy-start.21 = (f32[3,256]{1,0:T(4,128)S(1)}, f32[3,256]{1,0:T(4,128)}, u32[]{:S(2)}) copy-start(f32[3,256]{1,0:T(4,128)} %copy-done.20) | copy-start | bytes 9220
  368.7 5.2 %copy-start.23 = (f32[3,256]{1,0:T(4,128)S(1)}, f32[3,256]{1,0:T(4,128)}, u32[]{:S(2)}) copy-start(f32[3,256]{1,0:T(4,128)} %copy-done.22) | copy-start | bytes 9220
  368.7 5.2 %copy-start.25 = (f32[3,256]{1,0:T(4,128)S(1)}, f32[3,256]{1,0:T(4,128)}, u32[]{:S(2)}) copy-start(f32[3,256]{1,0:T(4,128)} %copy-done.24) | copy-start | bytes 9220
  368.7 5.2 %copy-start.27 = (f32[3,256]{1,0:T(4,128)S(1)}, f32[3,256]{1,0:T(4,128)}, u32[]{:S(2)}) copy-start(f32[3,256]{1,0:T(4,128)} %copy-done.26) | copy-start | bytes 9220
  368.7 5.2 %copy-start.29 = (f32[1,3,256]{2,1,0:T(4,128)S(1)}, f32[1,3,256]{2,1,0:T(4,128)}, u32[]{:S(2)}) copy-start(f32[1,3,256]{2,1,0:T(4,128)} %copy-done.28) | copy-start | bytes 9220
  368.8 5.0 %collective-permute-start.1 = (bf16[3,6,256]{2,1,0:T(8,128)(2,1)S(1)}, bf16[3,6,256]{2,1,0:T(8,128)(2,1)S(1)}, u32[]{:S(2)}, u32[]{:S(2)}) collective-permute-start(bf16[3,6,256]{2,1,0:T(8,128)(2,1)S(1)} %pad_maximum_fusion.12), channel_id=1, source_target_pairs={{16,0},{32,16},{48,32},{64,48},{80,64},{96,80},{112,96},{128,112},... | collective-permute-start | bytes 27656 | tf_op jit(solution)/shard_map/ppermute | solution.py:14
  (3 other events, 5.3 us)
Sparse Core Ops, SparseCore 0:
  11.0 66.2 all-gather.1
  367.9 81.9 reduce-scatter.1
where the time goes:
time: 464 us; the launch traced here: 458 us
  waiting for transfers between devices  145 us (31%)
  local copies, waits for them, and re-layouts  144 us (31%)
  blocking collectives  72.4 us (16%)
  other arithmetic  40 us (9%)
  starting transfers between devices  22.9 us (5%)
  matrix products  19.7 us (4%)
  between operations  15 us (3%)
    reduce_scatter x1, waiting for transfers between devices, shards(): lax.psum_scatter(partial_proj, 'ch', scatter_dimension=1, tiled=True)  74.6 us
    all_gather x1, waiting for transfers between devices, shards(): lax.all_gather(out_grad, 'ch', axis=1, tiled=True)  56 us
    pad x20, local copies, waits for them, and re-layouts, prepare(): lax.associative_scan(combine, (block_final_states, factor), axis=1)  42.8 us
    slice x34, local copies, waits for them, and re-layouts, prepare(): lax.associative_scan(combine, (block_final_states, factor), axis=1)  32.8 us
    all_to_all x1, blocking collectives, long_backward(): lax.all_to_all(final_output, 'ctx', split_axis=1, concat_axis=0, tiled=True)  26.5 us
    all_to_all x1, blocking collectives, long_forward(): lax.all_to_all(final_output, 'ctx', split_axis=1, concat_axis=0, tiled=True)  25.9 us
    rev x1, local copies, waits for them, and re-layouts, long_backward(): jnp.flip(finish(within_block, running, decays, jnp.zeros(decays.shape, jn...  24 us
    rev x1, local copies, waits for them, and re-layouts, long_backward(): jnp.flip(sequence.astype(jnp.float32), 1)  21.2 us
  transfers between devices with their start and end apart: 5, of which 4 were waited for; matrix products, arithmetic and copies ran while one was open for 3% of the time, Pallas kernels for 0%

commit v1 on v0

v1 whole, which is shorter than its diff:
```python
import functools

import jax
import jax.numpy as jnp
from jax import lax
from jax.experimental import pallas as pl
from jax.experimental.pallas import tpu as pltpu
from jax.sharding import PartitionSpec as P

MESH = pl.DeviceIdType.MESH
F32 = jnp.float32
BF16 = jnp.bfloat16
SIDE = 4
SUB = 8
LANES = 128
AG_COPIES = 44
RS_COPIES = 60


def kernel(
    chips,
    modes,
    taps_len,
    q_in,
    k_in,
    v_in,
    taps_in,
    res_in,
    dec_in,
    w_in,
    g_in,
    proj_out,
    gq_out,
    gk_out,
    gv_out,
    raw,
    taps,
    res,
    dec,
    weight,
    gathered,
    halo,
    natural,
    extended,
    feats,
    signal,
    conv,
    gradient,
    filt,
    small,
    rates,
    decay,
    scan_buf,
    prefix,
    s_send,
    s_recv,
    x_send,
    x_recv,
    carry,
    gate,
    keep0,
    keep1,
    send_a,
    send_p,
    send_b,
    recv_a,
    recv_p,
    recv_b,
    part2,
    own2,
    send2_b,
    recv2_a,
    recv2_p,
    recv2_b,
    gfeats,
    edge_send,
    edge_recv,
    outs,
    local_sem,
    ag_send,
    ag_recv,
    rs_send,
    rs_recv,
    z_send,
    z_recv,
    p_send,
    p_recv,
    h_send,
    h_recv,
    e_send,
    e_recv,
    out_sem,
):
    length, width = q_in.shape
    rows = length // SUB
    half = length // 2
    quarter = length // 4
    lanes = range(width // LANES)
    ctx = lax.axis_index("ctx")
    ch = lax.axis_index("ch")
    z, core = ctx // 2, ctx % 2
    x, y = ch // SIDE, ch % SIDE
    n_ctx = 2 * chips
    before = (ctx + n_ctx - 1) % n_ctx
    after = (ctx + 1) % n_ctx
    partner = z * 2 + (1 - core)

    def plane(axis, step):
        if axis == 0:
            other = ((x + step) % SIDE) * SIDE + y
        else:
            other = x * SIDE + (y + step) % SIDE
        return {"ctx": ctx, "ch": other}

    def along_z(step):
        return {"ctx": ((z + step) % chips) * 2 + core, "ch": ch}

    def at_ctx(other):
        return {"ctx": other, "ch": ch}

    local = [
        pltpu.make_async_copy(dec_in, dec, local_sem.at[0]),
        pltpu.make_async_copy(res_in, res, local_sem.at[1]),
        pltpu.make_async_copy(taps_in, taps, local_sem.at[2]),
        pltpu.make_async_copy(q_in, raw.at[0], local_sem.at[3]),
        pltpu.make_async_copy(k_in, raw.at[1], local_sem.at[4]),
        pltpu.make_async_copy(v_in, raw.at[2], local_sem.at[5]),
        pltpu.make_async_copy(g_in, gathered.at[0, 0], local_sem.at[6]),
        pltpu.make_async_copy(w_in, weight, local_sem.at[7]),
    ]
    for copy in local:
        copy.start()

    barrier = pltpu.get_barrier_semaphore()
    peers = [plane(0, 1), plane(0, -1), plane(1, 1), plane(1, -1), at_ctx(before), at_ctx(after)]
    peers += [along_z(step) for step in range(1, chips)]
    for peer in peers:
        pl.semaphore_signal(barrier, inc=1, device_id=peer, device_id_type=MESH)
    pl.semaphore_wait(barrier, len(peers))

    def remote(src, dst, sends, recvs, index, device):
        return pltpu.make_async_remote_copy(
            src_ref=src,
            dst_ref=dst,
            send_sem=sends.at[index],
            recv_sem=recvs.at[index],
            device_id=device,
            device_id_type=MESH,
        )

    ag = {}

    def slot(h, i, j):
        return gathered.at[i, j] if h == 0 else gathered.at[j, i]

    def piece(ref, h, part):
        if part is None:
            return ref.at[pl.ds(h * half, half)]
        return ref.at[pl.ds(h * half + part * quarter, quarter)]

    def ag_copy(h, phase, source, i, j, part, step):
        key = (h, i, j, part, step)
        index = len(ag)
        axis = phase if h == 0 else 1 - phase
        copy = remote(
            piece(source, h, part), piece(slot(h, i, j), h, part), ag_send, ag_recv, index, plane(axis, step)
        )
        ag[key] = copy
        copy.start()

    def ag_wait(h, i, j, part, step):
        ag[(h, i, j, part, step)].wait_recv()

    for h in range(2):
        for step in (1, -1):
            ag_copy(h, 0, g_in, step % SIDE, 0, None, step)
    for s in range(3):
        remote(
            (q_in, k_in, v_in)[s].at[pl.ds(length - 16, 16)], halo.at[s], h_send, h_recv, s, at_ctx(after)
        ).start()
    for h in range(2):
        for step in (1, -1):
            ag_copy(h, 1, g_in, 0, step % SIDE, None, step)

    def ag_relay1():
        for h in range(2):
            for step in (1, -1):
                i = step % SIDE
                ag_wait(h, i, 0, None, step)
                ag_copy(h, 0, slot(h, i, 0), 2, 0, 0 if step == 1 else 1, step)
        for h in range(2):
            for i in (1, 3):
                for step in (1, -1):
                    ag_copy(h, 1, slot(h, i, 0), i, step % SIDE, None, step)

    def ag_relay2(i):
        for h in range(2):
            for step in (1, -1):
                j = step % SIDE
                ag_wait(h, i, j, None, step)
                ag_copy(h, 1, slot(h, i, j), i, 2, 0 if step == 1 else 1, step)

    def ag_far():
        for h in range(2):
            for part, step in ((0, 1), (1, -1)):
                ag_wait(h, 2, 0, part, step)
                for to in (1, -1):
                    ag_copy(h, 1, slot(h, 2, 0), 2, to % SIDE, part, to)

    def ag_relay_far():
        for h in range(2):
            for step in (1, -1):
                part = 0 if step == 1 else 1
                ag_wait(h, 2, step % SIDE, part, step)
                ag_copy(h, 1, slot(h, 2, step % SIDE), 2, 2, part, step)

    def ag_last():
        for h in range(2):
            for step in (1, -1):
                ag_wait(h, 2, step % SIDE, 1 if step == 1 else 0, step)
        for i in (0, 1, 3, 2):
            for h in range(2):
                for part, step in ((0, 1), (1, -1)):
                    ag_wait(h, i, 2, part, step)

    local[0].wait()
    local[1].wait()
    rates[0] = jnp.transpose(dec[...])
    rates[1] = jnp.transpose(res[...])
    rate = rates[0]
    scale = rates[1] * jnp.sqrt(rate)
    rates[1] = scale
    offsets = lax.broadcasted_iota(jnp.int32, (rows, width), 0).astype(F32)
    total = jnp.zeros((rows, width), F32)
    for n in range(modes):
        total = total + rates[1, n : n + 1, :] * jnp.exp(-rates[0, n : n + 1, :] * offsets)
    small[...] = total
    for d in range(rows):
        filt[d] = jnp.broadcast_to(small[d : d + 1, :], (SUB, width))
    for n in range(modes):
        own = jnp.broadcast_to(rates[0, n : n + 1, :], (SUB, width))
        decay[6, n] = jnp.broadcast_to(rates[1, n : n + 1, :], (SUB, width))
        decay[0, n] = jnp.exp(-own)
        step_decay = jnp.exp(-own * rows)
        decay[1, n] = step_decay
        step_decay = step_decay * step_decay
        decay[2, n] = step_decay
        step_decay = step_decay * step_decay
        decay[3, n] = step_decay
        place = lax.broadcasted_iota(jnp.int32, (SUB, width), 0)
        decay[4, n] = jnp.exp(-own * (rows * place).astype(F32))
        decay[5, n] = jnp.exp(-own * (rows * (SUB - 1 - place)).astype(F32))
    block_decay = jnp.exp(-rate * length)
    pair_decay = jnp.exp(-rate * (2 * length))
    sublane = lax.broadcasted_iota(jnp.int32, (modes, SUB, width), 1)

    def states(signal, direction):
        def advance(r, total):
            at = r if direction == 1 else rows - 1 - r
            return total * decay[0] + signal[at][None]

        total = lax.fori_loop(0, rows, advance, jnp.zeros((modes, SUB, width), F32))
        for level, step in enumerate((1, 2, 4)):
            if direction == 1:
                moved = jnp.where(sublane >= step, pltpu.roll(total, step, 1), 0.0)
            else:
                moved = jnp.where(sublane < SUB - step, pltpu.roll(total, SUB - step, 1), 0.0)
            total = total + decay[1 + level] * moved
        if direction == 1:
            prefix[...] = jnp.where(sublane >= 1, pltpu.roll(total, 1, 1), 0.0)
        else:
            prefix[...] = jnp.where(sublane < SUB - 1, pltpu.roll(total, SUB - 1, 1), 0.0)
        scan_buf[...] = total
        edge = SUB - 1 if direction == 1 else 0
        for n in range(modes):
            carry[0, n : n + 1, :] = scan_buf[n, edge : edge + 1, :]

    def send_states(way, direction):
        s_send[way] = carry[0].astype(BF16)
        for step in range(chips // 2, 0, -1):
            for distance in {step, chips - step}:
                remote(
                    s_send.at[way],
                    s_recv.at[way, distance],
                    z_send.at[way],
                    z_recv.at[way],
                    distance,
                    along_z(direction * distance),
                ).start()

    def take_states(way, direction):
        total = jnp.zeros((modes, width), F32)
        for distance in range(chips - 1, 0, -1):
            remote(
                s_send.at[way],
                s_recv.at[way, distance],
                z_send.at[way],
                z_recv.at[way],
                distance,
                along_z(direction * distance),
            ).wait_recv()
            source = z - distance if direction == 1 else chips - 1 - z - distance
            there = (source >= 0).astype(F32)
            total = total * pair_decay + there * s_recv[way, distance].astype(F32)
        leads = (core == 0) if direction == 1 else (core == 1)
        leads = leads.astype(F32)
        x_send[way] = leads * (pair_decay * total + carry[0]) + (1.0 - leads) * total
        copy = remote(x_send.at[way], x_recv.at[way], p_send, p_recv, way, at_ctx(partner))
        copy.start()
        carry[1] = block_decay * total

    def finish_states(way):
        remote(x_send.at[way], x_recv.at[way], p_send, p_recv, way, at_ctx(partner)).wait_recv()
        carry[1] = carry[1] + x_recv[way]
        for n in range(modes):
            scan_buf[n] = jnp.broadcast_to(carry[1, n : n + 1, :], (SUB, width))

    def carried(out, direction):
        reach = decay[4] if direction == 1 else decay[5]
        start = decay[6] * decay[0] * (prefix[...] + reach * scan_buf[...])

        def advance(r, state):
            at = r if direction == 1 else rows - 1 - r
            out[at] = out[at] + jnp.sum(state, axis=0)
            return state * decay[0]

        lax.fori_loop(0, rows, advance, start)

    ag_relay1()
    for index in (2, 3, 4, 5):
        local[index].wait()
    first = (ctx > 0).astype(F32)
    for s in range(3):
        remote(
            (q_in, k_in, v_in)[s].at[pl.ds(length - 16, 16)], halo.at[s], h_send, h_recv, s, at_ctx(after)
        ).wait_recv()
        for g in lanes:
            cols = slice(g * LANES, (g + 1) * LANES)
            natural[s, g, 8 : 8 + length] = raw[s, :, cols].astype(F32)
            natural[s, g, 0:8] = halo[s, :, cols].astype(F32)[8:16] * first
            for i in range(8 - taps_len + 1, 8 + rows):
                extended[s, i, :, cols] = natural[s, g, pl.ds(i, SUB, stride=rows), :]
        total = jnp.zeros((rows, SUB, width), F32)
        for j in range(taps_len):
            total = total + taps[j, s : s + 1, :][None] * extended[s, 8 - j : 8 - j + rows]
        feats[s] = total
    signal[...] = (feats[1] * feats[2]).astype(BF16).astype(F32)

    states(signal, 1)
    send_states(0, 1)
    ag_relay2(0)
    ag_far()
    conv[0] = filt[0][None] * signal[...]
    for d in range(1, rows):
        conv[0, d:rows] = conv[0, d:rows] + filt[d][None] * signal[0 : rows - d]
    ag_relay2(1)
    ag_relay2(3)
    ag_relay_far()
    take_states(0, 1)
    finish_states(0)
    carried(conv.at[0], 1)
    gate[...] = (feats[0] * conv[0]).astype(BF16).reshape(length, width)

    local[7].wait()
    rs = {}

    def rs_copy(key, src, dst, axis, step):
        copy = remote(src, dst, rs_send, rs_recv, len(rs), plane(axis, step))
        rs[key] = copy
        copy.start()

    def first_axis(h):
        return 1 if h == 0 else 0

    lower, upper = pl.ds(0, quarter), pl.ds(quarter, quarter)

    def terms(dx, dy):
        dest = ((x + dx) % SIDE) * SIDE + (y + dy) % SIDE
        product = jnp.dot(
            gate[...],
            weight[:, pl.ds(pl.multiple_of(dest * width, width), width)],
            preferred_element_type=F32,
        )
        for h in range(2):
            i, j = (dx, dy) if h == 0 else (dy, dx)
            own = product[h * half : (h + 1) * half]
            if j == 2:
                send_a[h, i] = own.astype(BF16)
                rs_copy(("a", h, i, 0), send_a.at[h, i, lower], recv_a.at[h, 0, i], first_axis(h), 1)
                rs_copy(("a", h, i, 1), send_a.at[h, i, upper], recv_a.at[h, 1, i], first_axis(h), -1)
            elif j == 1:
                keep1[h, 0, i] = own[:quarter]
                send_p[h, 0, i] = own[quarter:].astype(BF16)
            elif j == 3:
                keep1[h, 1, i] = own[quarter:]
                send_p[h, 1, i] = own[:quarter].astype(BF16)
            else:
                keep0[h, i] = own

    for dx, dy in ((2, 2), (2, 1), (1, 2), (2, 3), (3, 2), (2, 0), (0, 2)):
        terms(dx, dy)
    for dx, dy in ((1, 1), (1, 3), (3, 1), (3, 3), (0, 1), (1, 0), (0, 3), (3, 0), (0, 0)):
        terms(dx, dy)

    ag_last()
    local[6].wait()
    grad = jnp.zeros((length, width), F32)
    for dx in range(SIDE):
        for dy in range(SIDE):
            source = ((x + SIDE - dx) % SIDE) * SIDE + (y + SIDE - dy) % SIDE
            grad = grad + lax.dot_general(
                gathered[dx, dy],
                weight[:, pl.ds(pl.multiple_of(source * width, width), width)],
                (((1,), (1,)), ((), ())),
                preferred_element_type=F32,
            )
    for g in lanes:
        cols = slice(g * LANES, (g + 1) * LANES)
        natural[0, g, 0:length] = grad[:, cols]
        for r in range(rows):
            gradient[r, :, cols] = natural[0, g, pl.ds(r, SUB, stride=rows), :]
    signal[...] = (gradient[...] * feats[0]).astype(BF16).astype(F32)
    states(signal, -1)
    send_states(1, -1)

    for h in range(2):
        for i in (2, 1, 3, 0):
            rs_copy(("p", h, i, 0), send_p.at[h, 0, i], recv_p.at[h, 0, i], first_axis(h), 1)
            rs_copy(("p", h, i, 1), send_p.at[h, 1, i], recv_p.at[h, 1, i], first_axis(h), -1)

    def rs_second():
        for i in (2, 1, 3, 0):
            for h in range(2):
                for way, step in ((0, 1), (1, -1)):
                    rs[("a", h, i, way)].wait_recv()
                    send_b[h, way, i] = (keep1[h, way, i] + recv_a[h, way, i].astype(F32)).astype(BF16)
                    rs_copy(("b", h, i, way), send_b.at[h, way, i], recv_b.at[h, way, i], first_axis(h), step)

    rs_second()

    conv[1] = filt[0][None] * signal[...]
    for d in range(1, rows):
        conv[1, 0 : rows - d] = conv[1, 0 : rows - d] + filt[d][None] * signal[d:rows]

    def edges(s):
        for j in range(16):
            small[j : j + 1, :] = gfeats[s, j, 0:1, :]
        edge_send[s] = small[0:16].astype(BF16)
        remote(edge_send.at[s], edge_recv.at[s], e_send, e_recv, s, at_ctx(before)).start()

    gfeats[0, 0:rows] = (gradient[...] * conv[0]).astype(BF16).astype(F32)
    edges(0)

    def collect(h, i):
        for way in range(2):
            rs[("p", h, i, way)].wait_recv()
            rs[("b", h, i, way)].wait_recv()
        low = keep0[h, i, 0:quarter] + recv_b[h, 0, i].astype(F32) + recv_p[h, 1, i].astype(F32)
        high = keep0[h, i, quarter:half] + recv_p[h, 0, i].astype(F32) + recv_b[h, 1, i].astype(F32)
        return low, high

    for h in range(2):
        axis = 1 - first_axis(h)
        low, high = collect(h, 2)
        part2[h, 0] = low.astype(BF16)
        part2[h, 1] = high.astype(BF16)
        rs_copy(("a2", h, 0), part2.at[h, 0], recv2_a.at[h, 0], axis, 1)
        rs_copy(("a2", h, 1), part2.at[h, 1], recv2_a.at[h, 1], axis, -1)
    for h in range(2):
        axis = 1 - first_axis(h)
        low, high = collect(h, 1)
        own2[h, 0] = low
        part2[h, 2] = high.astype(BF16)
        rs_copy(("p2", h, 0), part2.at[h, 2], recv2_p.at[h, 0], axis, 1)
        low, high = collect(h, 3)
        own2[h, 1] = high
        part2[h, 3] = low.astype(BF16)
        rs_copy(("p2", h, 1), part2.at[h, 3], recv2_p.at[h, 1], axis, -1)
    for h in range(2):
        axis = 1 - first_axis(h)
        low, high = collect(h, 0)
        own2[h, 2] = low
        own2[h, 3] = high
        for way, step in ((0, 1), (1, -1)):
            rs[("a2", h, way)].wait_recv()
            send2_b[h, way] = (own2[h, way] + recv2_a[h, way].astype(F32)).astype(BF16)
            rs_copy(("b2", h, way), send2_b.at[h, way], recv2_b.at[h, way], axis, step)

    take_states(1, -1)
    finish_states(1)
    carried(conv.at[1], -1)
    gfeats[1, 0:rows] = (conv[1] * feats[2]).astype(BF16).astype(F32)
    edges(1)
    gfeats[2, 0:rows] = (conv[1] * feats[1]).astype(BF16).astype(F32)
    edges(2)

    for h in range(2):
        for way in range(2):
            rs[("p2", h, way)].wait_recv()
            rs[("b2", h, way)].wait_recv()
        low = own2[h, 2] + recv2_b[h, 0].astype(F32) + recv2_p[h, 1].astype(F32)
        high = own2[h, 3] + recv2_p[h, 0].astype(F32) + recv2_b[h, 1].astype(F32)
        per = quarter // SUB
        for piece_index, value in ((2 * h, low), (2 * h + 1, high)):
            value = value.reshape(per, SUB, width)
            for g in lanes:
                for r in range(per):
                    natural[1, g, pl.ds(piece_index * per + r, SUB, stride=rows), :] = value[
                        r, :, g * LANES : (g + 1) * LANES
                    ]
    for g in lanes:
        outs[0, :, g * LANES : (g + 1) * LANES] = natural[1, g, 0:length].astype(BF16)
    out_copies = [pltpu.make_async_copy(outs.at[0], proj_out, out_sem.at[0])]
    out_copies[0].start()

    last = (ctx < n_ctx - 1).astype(F32)
    place = lax.broadcasted_iota(jnp.int32, (SUB, width), 0)
    for s in range(3):
        remote(edge_send.at[s], edge_recv.at[s], e_send, e_recv, s, at_ctx(before)).wait_recv()
        small[0:16] = edge_recv[s].astype(F32) * last
        for j in range(taps_len - 1):
            moved = pltpu.roll(gfeats[s, j], SUB - 1, 0)
            gfeats[s, rows + j] = jnp.where(
                place == SUB - 1, jnp.broadcast_to(small[j : j + 1, :], (SUB, width)), moved
            )
        total = jnp.zeros((rows, SUB, width), F32)
        for j in range(taps_len):
            total = total + taps[j, s : s + 1, :][None] * gfeats[s, j : j + rows]
        for g in lanes:
            cols = slice(g * LANES, (g + 1) * LANES)
            for r in range(rows):
                natural[2, g, pl.ds(r, SUB, stride=rows), :] = total[r, :, cols]
            outs[1 + s, :, cols] = natural[2, g, 0:length].astype(BF16)
        copy = pltpu.make_async_copy(outs.at[1 + s], (gq_out, gk_out, gv_out)[s], out_sem.at[1 + s])
        copy.start()
        out_copies.append(copy)

    for copy in ag.values():
        copy.wait_send()
    for copy in rs.values():
        copy.wait_send()
    for s in range(3):
        remote(
            (q_in, k_in, v_in)[s].at[pl.ds(length - 16, 16)], halo.at[s], h_send, h_recv, s, at_ctx(after)
        ).wait_send()
        remote(edge_send.at[s], edge_recv.at[s], e_send, e_recv, s, at_ctx(before)).wait_send()
    for way, direction in ((0, 1), (1, -1)):
        for distance in range(1, chips):
            remote(
                s_send.at[way],
                s_recv.at[way, distance],
                z_send.at[way],
                z_recv.at[way],
                distance,
                along_z(direction * distance),
            ).wait_send()
        remote(x_send.at[way], x_recv.at[way], p_send, p_recv, way, at_ctx(partner)).wait_send()
    for copy in out_copies:
        copy.wait()


def shards(query_in, key_in, value_in, short_taps, residues, decays, out_weight, out_grad):
    length, width = query_in.shape
    rows = length // SUB
    half, quarter = length // 2, length // 4
    taps_len = short_taps.shape[0]
    modes = decays.shape[1]
    chips = lax.axis_size("ctx") // 2
    vmem = pltpu.VMEM
    dma = pltpu.SemaphoreType.DMA
    scratch = [
        vmem((3, length, width), BF16),
        vmem(short_taps.shape, F32),
        vmem(residues.shape, F32),
        vmem(decays.shape, F32),
        vmem(out_weight.shape, BF16),
        vmem((SIDE, SIDE, length, width), BF16),
        vmem((3, 16, width), BF16),
        vmem((3, width // LANES, length + 8, LANES), F32),
        vmem((3, rows + 8, SUB, width), F32),
        vmem((3, rows, SUB, width), F32),
        vmem((rows, SUB, width), F32),
        vmem((2, rows, SUB, width), F32),
        vmem((rows, SUB, width), F32),
        vmem((rows, SUB, width), F32),
        vmem((rows, width), F32),
        vmem((2, modes, width), F32),
        vmem((7, modes, SUB, width), F32),
        vmem((modes, SUB, width), F32),
        vmem((modes, SUB, width), F32),
        vmem((2, modes, width), BF16),
        vmem((2, chips, modes, width), BF16),
        vmem((2, modes, width), F32),
        vmem((2, modes, width), F32),
        vmem((2, modes, width), F32),
        vmem((length, width), BF16),
        vmem((2, SIDE, half, width), F32),
        vmem((2, 2, SIDE, quarter, width), F32),
        vmem((2, SIDE, half, width), BF16),
        vmem((2, 2, SIDE, quarter, width), BF16),
        vmem((2, 2, SIDE, quarter, width), BF16),
        vmem((2, 2, SIDE, quarter, width), BF16),
        vmem((2, 2, SIDE, quarter, width), BF16),
        vmem((2, 2, SIDE, quarter, width), BF16),
        vmem((2, 4, quarter, width), BF16),
        vmem((2, 4, quarter, width), F32),
        vmem((2, 2, quarter, width), BF16),
        vmem((2, 2, quarter, width), BF16),
        vmem((2, 2, quarter, width), BF16),
        vmem((2, 2, quarter, width), BF16),
        vmem((3, rows + 8, SUB, width), F32),
        vmem((3, 16, width), BF16),
        vmem((3, 16, width), BF16),
        vmem((4, length, width), BF16),
        dma((8,)),
        dma((AG_COPIES,)),
        dma((AG_COPIES,)),
        dma((RS_COPIES,)),
        dma((RS_COPIES,)),
        dma((2, chips)),
        dma((2, chips)),
        dma((2,)),
        dma((2,)),
        dma((3,)),
        dma((3,)),
        dma((3,)),
        dma((3,)),
        dma((4,)),
    ]
    out = jax.ShapeDtypeStruct((length, width), BF16)
    return pl.pallas_call(
        functools.partial(kernel, chips, modes, taps_len),
        out_shape=(out, out, out, out),
        in_specs=[pl.BlockSpec(memory_space=pl.ANY)] * 8,
        out_specs=[pl.BlockSpec(memory_space=pl.ANY)] * 4,
        scratch_shapes=scratch,
        compiler_params=pltpu.CompilerParams(
            collective_id=0, has_side_effects=True, vmem_limit_bytes=56 * 1024 * 1024
        ),
        name="hyena",
    )(query_in, key_in, value_in, short_taps, residues, decays, out_weight, out_grad)


def solution(mesh):
    in_specs = (
        P("ctx", "ch"),
        P("ctx", "ch"),
        P("ctx", "ch"),
        P(None, None, "ch"),
        P("ch", None),
        P("ch", None),
        P("ch", None),
        P("ctx", "ch"),
    )
    out_specs = (P("ctx", "ch"), P("ctx", "ch"), P("ctx", "ch"), P("ctx", "ch"))
    return jax.shard_map(shards, mesh=mesh, in_specs=in_specs, out_specs=out_specs, check_vma=False)
```

time: 464 us -> 66.3 us (0.14); the launches traced: 458 us -> 66 us
  waiting for transfers between devices: 145 us -> 0 us
  local copies, waits for them, and re-layouts: 144 us -> 10.6 us
  blocking collectives: 72.4 us -> 0 us
  Pallas kernels: 0 us -> 54.8 us
  other arithmetic: 40 us -> 0 us
  starting transfers between devices: 22.9 us -> 0 us
  matrix products: 19.7 us -> 0 us
  between operations: 15 us -> 0.64 us
    reduce_scatter x1 -> x0, waiting for transfers between devices: 74.6 us -> none  [shards(): lax.psum_scatter(partial_proj, 'ch', scatter_dimension=1, tiled=True)]
    all_to_all x3 -> x0, blocking collectives: 72.4 us -> none  [the longest x1 26.5 us: long_backward(): lax.all_to_all(final_output, 'ctx', split_axis=1, concat_axis=0, tiled=True)]
    all_gather x1 -> x0, waiting for transfers between devices: 56 us -> none  [shards(): lax.all_gather(out_grad, 'ch', axis=1, tiled=True)]
    pallas_call x0 -> x1, Pallas kernels: none -> 54.8 us  [shards(): pl.pallas_call(functools.partial(kernel, chips, modes, taps_len), out_sha...]
    rev x2 -> x0, local copies, waits for them, and re-layouts: 45.1 us -> none  [the longest x1 24 us: long_backward(): jnp.flip(finish(within_block, running, decays, jnp.zeros(decays.shape, jn...]
    pad x20 -> x0, local copies, waits for them, and re-layouts: 42.8 us -> none  [prepare(): lax.associative_scan(combine, (block_final_states, factor), axis=1)]
    slice x37 -> x0, local copies, waits for them, and re-layouts: 37.1 us -> none  [the longest x34 32.8 us: prepare(): lax.associative_scan(combine, (block_final_states, factor), axis=1)]
    add x40 -> x0, other arithmetic: 27.6 us -> none  [the longest x24 20 us: combine(): return (earlier[0] * latter[1] + latter[0], earlier[1] * latter[1])]
  transfers between devices with their start and end apart: 5 -> 0, of which waited for: 4 -> 0; matrix products, arithmetic and copies ran while one was open for 3% -> 0% of each run, Pallas kernels for 0% -> 0%
where the time goes in v1:
time: 66.3 us; the launch traced here: 66 us
  Pallas kernels  54.8 us (83%)
  local copies, waits for them, and re-layouts  10.6 us (16%)
    pallas_call x1, Pallas kernels, shards(): pl.pallas_call(functools.partial(kernel, chips, modes, taps_len), out_sha...  54.8 us
    unnamed x7, local copies, waits for them, and re-layouts  10.6 us

profile of v1, /device:TPU:1, one launch (start us, length us, event | category | flops | bytes accessed | tf_op | source)
XLA Modules:
  0.0 66.0 jit_solution(12772746901492102942)
XLA Ops:
  0.6 1.4 %copy.12.taps_in = f32[7,3,256]{2,1,0:T(4,128)} copy(f32[7,3,256]{2,0,1:T(8,128)} %param.11) | data formatting | bytes 43008 | tf_op args[3]
  2.0 1.5 %copy.13.res_in = f32[256,16]{1,0:T(8,128)} copy(f32[256,16]{0,1:T(8,128)} %param.12) | data formatting | bytes 32768 | tf_op args[4]
  3.5 1.5 %copy.14.dec_in = f32[256,16]{1,0:T(8,128)} copy(f32[256,16]{0,1:T(8,128)} %param.13) | data formatting | bytes 32768 | tf_op args[5]
  4.9 54.8 %hyena.1 = (bf16[256,256]{1,0:T(8,128)(2,1)}, bf16[256,256]{1,0:T(8,128)(2,1)}, bf16[256,256]{1,0:T(8,128)(2,1)}, bf16[256,256]{1,0:T(8,128)(2,1)}) custom-call(bf16[256,256]{1,0:T(8,128)(2,1)} %q_in.1, bf16[256,256]{1,0:T(8,128)(2,1)} %k_in.1, bf16[256,256]{1,0:T(8,128)(2,1)} %v_in.1, f32[7,3,256]{2,1,0:T(4,128)} %copy.12.taps_in, f32[256,16]{1,0:T(8,128)} %copy.13.res_in, ...), custom_call_target="tpu_custom_call" | custom-call | tf_op jit(solution)/shard_map/hyena/pallas_call | solution.py:631
  59.7 1.6 %copy.19 = bf16[256,256]{1,0:T(8,128)(2,1)} copy(bf16[256,256]{1,0:T(8,128)(2,1)} %get-tuple-element.8) | data formatting | bytes 262144
  61.3 1.6 %copy.20 = bf16[256,256]{1,0:T(8,128)(2,1)} copy(bf16[256,256]{1,0:T(8,128)(2,1)} %get-tuple-element.9) | data formatting | bytes 262144
  62.8 1.6 %copy.21 = bf16[256,256]{1,0:T(8,128)(2,1)} copy(bf16[256,256]{1,0:T(8,128)(2,1)} %get-tuple-element.10) | data formatting | bytes 262144
  64.4 1.6 %copy.22 = bf16[256,256]{1,0:T(8,128)(2,1)} copy(bf16[256,256]{1,0:T(8,128)(2,1)} %get-tuple-element.11) | data formatting | bytes 262144

commit v2 on v1

v2 whole, which is shorter than its diff:
```python
import functools

import jax
import jax.numpy as jnp
from jax import lax
from jax.experimental import pallas as pl
from jax.experimental.pallas import tpu as pltpu
from jax.sharding import PartitionSpec as P

MESH = pl.DeviceIdType.MESH
F32 = jnp.float32
BF16 = jnp.bfloat16
SIDE = 4
SUB = 8
SENDS, RECEIVES = 9, 62


def kernel(
    chips,
    modes,
    taps_len,
    q_in,
    k_in,
    v_in,
    taps_in,
    res_in,
    dec_in,
    w_in,
    g_in,
    proj_out,
    gq_out,
    gk_out,
    gv_out,
    raw,
    taps,
    res,
    dec,
    weight,
    gathered,
    halo,
    extended,
    feats,
    signal,
    conv,
    gradient,
    total_grad,
    filt,
    small,
    rates,
    decay,
    scan_buf,
    prefix,
    s_send,
    s_recv,
    x_send,
    x_recv,
    carry,
    gate,
    keep0,
    keep1,
    send_a,
    send_p,
    send_b,
    recv_a,
    recv_p,
    recv_b,
    part2,
    own2,
    send2_b,
    recv2_a,
    recv2_p,
    recv2_b,
    gfeats,
    edge_send,
    edge_recv,
    to_rows,
    to_tokens,
    local_sem,
    send_sem,
    recv_sem,
    ring_sem,
):
    length, width = q_in.shape
    rows = length // SUB
    half = length // 2
    quarter = length // 4
    ctx = lax.axis_index("ctx")
    ch = lax.axis_index("ch")
    z, core = ctx // 2, ctx % 2
    x, y = ch // SIDE, ch % SIDE
    n_ctx = 2 * chips
    before = (ctx + n_ctx - 1) % n_ctx
    after = (ctx + 1) % n_ctx
    partner = z * 2 + (1 - core)
    place = lax.broadcasted_iota(jnp.int32, (SUB, width), 0)

    def plane(axis, step):
        if axis == 0:
            other = ((x + step) % SIDE) * SIDE + y
        else:
            other = x * SIDE + (y + step) % SIDE
        return {"ctx": ctx, "ch": other}

    def along_z(step):
        return {"ctx": ((z + step) % chips) * 2 + core, "ch": ch}

    def at_ctx(other):
        return {"ctx": other, "ch": ch}

    barrier = pltpu.get_barrier_semaphore()
    peers = [plane(0, 1), plane(0, -1), plane(1, 1), plane(1, -1)]
    peers += [at_ctx(before), at_ctx(after)]
    peers += [along_z(step) for step in (1, -1, 2, -2)]
    for peer in peers:
        pl.semaphore_signal(barrier, inc=1, device_id=peer, device_id_type=MESH)

    local = [
        pltpu.make_async_copy(q_in, raw.at[0], local_sem.at[0]),
        pltpu.make_async_copy(k_in, raw.at[1], local_sem.at[1]),
        pltpu.make_async_copy(v_in, raw.at[2], local_sem.at[2]),
        pltpu.make_async_copy(dec_in, dec, local_sem.at[3]),
        pltpu.make_async_copy(res_in, res, local_sem.at[4]),
        pltpu.make_async_copy(taps_in, taps, local_sem.at[5]),
        pltpu.make_async_copy(g_in, gathered.at[0], local_sem.at[6]),
        pltpu.make_async_copy(w_in, weight, local_sem.at[7]),
    ]
    for copy in local:
        copy.start()
    pl.semaphore_wait(barrier, len(peers))

    slots, sent_on, sent = {}, {}, {}

    def slot_of(name):
        return slots.setdefault(name, len(slots))

    def send(key, group, src, dst, device):
        copy = pltpu.make_async_remote_copy(
            src_ref=src,
            dst_ref=dst,
            send_sem=send_sem.at[sent_on.setdefault(group, len(sent_on))],
            recv_sem=recv_sem.at[slot_of(key)],
            device_id=device,
            device_id_type=MESH,
        )
        sent.setdefault(key, []).append(copy)
        copy.start()

    def receive(*key, view=None):
        if view is None:
            (copy,) = sent[key]
            copy.wait_recv()
        else:
            pltpu.make_async_copy(view, view, recv_sem.at[slots[key]]).wait()

    def slot(h, i, j):
        return gathered.at[i * SIDE + j] if h == 0 else gathered.at[j * SIDE + i]

    def piece(ref, h, part):
        if part is None:
            return ref.at[pl.ds(h * half, half)]
        return ref.at[pl.ds(h * half + part * quarter, quarter)]

    def ag_copy(h, phase, source, i, j, part, step, key=None):
        axis = phase if h == 0 else 1 - phase
        send(
            ("ag", h, i, j, part, step) if key is None else key,
            "ag",
            piece(source, h, part),
            piece(slot(h, i, j), h, part),
            plane(axis, step),
        )

    def ag_wait(h, i, j, part, step):
        receive("ag", h, i, j, part, step)

    for h in range(2):
        for step in (1, -1):
            ag_copy(h, 0, g_in, step % SIDE, 0, None, step)
    for s in range(3):
        tail = (q_in, k_in, v_in)[s].at[pl.ds(length - 16, 16)]
        send(("halo",), "halo", tail, halo.at[s], at_ctx(after))
    for h in range(2):
        for step in (1, -1):
            ag_copy(h, 1, g_in, 0, step % SIDE, None, step)

    def ag_relay1():
        for h in range(2):
            for step in (1, -1):
                i = step % SIDE
                ag_wait(h, i, 0, None, step)
                ag_copy(h, 0, slot(h, i, 0), 2, 0, 0 if step == 1 else 1, step)
        for h in range(2):
            for i in (1, 3):
                for step in (1, -1):
                    ag_copy(h, 1, slot(h, i, 0), i, step % SIDE, None, step)

    def ag_relay2(i):
        for h in range(2):
            for step in (1, -1):
                j = step % SIDE
                ag_wait(h, i, j, None, step)
                ag_copy(h, 1, slot(h, i, j), i, 2, 0 if step == 1 else 1, step, ("last",))

    def ag_far():
        for h in range(2):
            for part, step in ((0, 1), (1, -1)):
                ag_wait(h, 2, 0, part, step)
                for to in (1, -1):
                    key = None if (part == 0) == (to == 1) else ("last",)
                    ag_copy(h, 1, slot(h, 2, 0), 2, to % SIDE, part, to, key)

    def ag_relay_far():
        for h in range(2):
            for step in (1, -1):
                part = 0 if step == 1 else 1
                ag_wait(h, 2, step % SIDE, part, step)
                ag_copy(h, 1, slot(h, 2, step % SIDE), 2, 2, part, step, ("last",))

    reaches = []
    while 2 * 2 ** len(reaches) < chips // 2:
        reaches.append(2 * 2 ** len(reaches))
    news = [0]

    def tell():
        if news[0] < len(reaches):
            for step in (reaches[news[0]], -reaches[news[0]]):
                pl.semaphore_signal(ring_sem.at[news[0]], inc=1, device_id=along_z(step), device_id_type=MESH)

    def pass_news():
        if news[0] < len(reaches):
            pl.semaphore_wait(ring_sem.at[news[0]], 2)
            news[0] += 1
            tell()

    tell()

    def one_hot(hit):
        return jnp.where(hit, 1.0, 0.0).astype(BF16)

    across = lax.broadcasted_iota(jnp.int32, (length, length), 1)
    down = lax.broadcasted_iota(jnp.int32, (length, length), 0)
    to_rows[...] = one_hot(across == (down % SUB) * rows + down // SUB)
    to_tokens[...] = one_hot(down == (across % SUB) * rows + across // SUB)

    def inner_order(value):
        return jnp.dot(to_rows[...], value, preferred_element_type=F32).reshape(rows, SUB, width)

    def token_order(value):
        return jnp.dot(to_tokens[...], value, preferred_element_type=F32).astype(BF16)

    local[3].wait()
    local[4].wait()
    rate = dec[...]
    rates[0] = rate
    rates[1] = res[...] * jnp.sqrt(rate)
    offsets = lax.broadcasted_iota(jnp.int32, (rows, width), 0).astype(F32)
    total = jnp.zeros((rows, width), F32)
    for n in range(modes):
        total = total + rates[1, n : n + 1, :] * jnp.exp(-rates[0, n : n + 1, :] * offsets)
    small[...] = total
    for d in range(rows):
        filt[d] = jnp.broadcast_to(small[d : d + 1, :], (SUB, width))
    for n in range(modes):
        own = jnp.broadcast_to(rates[0, n : n + 1, :], (SUB, width))
        decay[6, n] = jnp.broadcast_to(rates[1, n : n + 1, :], (SUB, width))
        decay[0, n] = jnp.exp(-own)
        step_decay = jnp.exp(-own * rows)
        decay[1, n] = step_decay
        step_decay = step_decay * step_decay
        decay[2, n] = step_decay
        step_decay = step_decay * step_decay
        decay[3, n] = step_decay
        decay[4, n] = jnp.exp(-own * (rows * place).astype(F32))
        decay[5, n] = jnp.exp(-own * (rows * (SUB - 1 - place)).astype(F32))
    block_decay = jnp.exp(-rate * length)
    pair_decay = jnp.exp(-rate * (2 * length))
    sublane = lax.broadcasted_iota(jnp.int32, (modes, SUB, width), 1)
    pass_news()

    def states(signal, direction):
        def advance(r, total):
            at = r if direction == 1 else rows - 1 - r
            return total * decay[0] + signal[at][None]

        total = lax.fori_loop(0, rows, advance, jnp.zeros((modes, SUB, width), F32))
        for level, step in enumerate((1, 2, 4)):
            if direction == 1:
                moved = jnp.where(sublane >= step, pltpu.roll(total, step, 1), 0.0)
            else:
                moved = jnp.where(sublane < SUB - step, pltpu.roll(total, SUB - step, 1), 0.0)
            total = total + decay[1 + level] * moved
        if direction == 1:
            prefix[...] = jnp.where(sublane >= 1, pltpu.roll(total, 1, 1), 0.0)
        else:
            prefix[...] = jnp.where(sublane < SUB - 1, pltpu.roll(total, SUB - 1, 1), 0.0)
        scan_buf[...] = total
        edge = SUB - 1 if direction == 1 else 0
        for n in range(modes):
            carry[0, n : n + 1, :] = scan_buf[n, edge : edge + 1, :]

    def send_states(way, direction):
        s_send[way] = carry[0].astype(BF16)
        for step in range(chips // 2, 0, -1):
            for distance in sorted({step, chips - step}):
                send(
                    ("z", way),
                    ("z", way),
                    s_send.at[way],
                    s_recv.at[way, distance - 1],
                    along_z(direction * distance),
                )

    def take_states(way, direction):
        receive("z", way, view=s_recv.at[way])
        total = jnp.zeros((modes, width), F32)
        for distance in range(chips - 1, 0, -1):
            source = z - distance if direction == 1 else chips - 1 - z - distance
            there = (source >= 0).astype(F32)
            total = total * pair_decay + there * s_recv[way, distance - 1].astype(F32)
        leads = (core == 0) if direction == 1 else (core == 1)
        leads = leads.astype(F32)
        x_send[way] = leads * (pair_decay * total + carry[0]) + (1.0 - leads) * total
        send(("x", way), ("x", way), x_send.at[way], x_recv.at[way], at_ctx(partner))
        carry[1] = block_decay * total

    def finish_states(way):
        receive("x", way)
        carry[1] = carry[1] + x_recv[way]
        for n in range(modes):
            scan_buf[n] = jnp.broadcast_to(carry[1, n : n + 1, :], (SUB, width))

    def carried_start(direction):
        reach = decay[4] if direction == 1 else decay[5]
        return decay[6] * decay[0] * (prefix[...] + reach * scan_buf[...])

    def carried(out, start, direction):
        def advance(r, state):
            at = r if direction == 1 else rows - 1 - r
            out[at] = out[at] + jnp.sum(state, axis=0)
            return state * decay[0]

        lax.fori_loop(0, rows, advance, start)

    for s in range(3):
        local[s].wait()
        extended[s, 8 : 8 + rows] = inner_order(raw[s])
    ag_relay1()
    local[5].wait()
    receive("halo", view=halo)
    first = (ctx > 0).astype(F32)
    for s in range(3):
        small[0:16] = halo[s].astype(F32) * first
        for j in range(1, taps_len):
            moved = pltpu.roll(extended[s, 8 + rows - j], 1, 0)
            extended[s, 8 - j] = jnp.where(
                place == 0, jnp.broadcast_to(small[16 - j : 17 - j, :], (SUB, width)), moved
            )
        total = jnp.zeros((rows, SUB, width), F32)
        for j in range(taps_len):
            total = total + taps[s, j : j + 1, :][None] * extended[s, 8 - j : 8 - j + rows]
        feats[s] = total
    signal[...] = (feats[1] * feats[2]).astype(BF16).astype(F32)

    states(signal, 1)
    while news[0] < len(reaches):
        pass_news()
    send_states(0, 1)
    ag_relay2(0)
    ag_far()

    conv[0] = filt[0][None] * signal[...]
    for d in range(1, rows):
        conv[0, d:rows] = conv[0, d:rows] + filt[d][None] * signal[0 : rows - d]
    ag_relay2(1)
    ag_relay2(3)

    def grad_terms(blocks):
        total = None
        for dx, dy in blocks:
            source = ((x + SIDE - dx) % SIDE) * SIDE + (y + SIDE - dy) % SIDE
            term = lax.dot_general(
                gathered[dx * SIDE + dy],
                weight[:, pl.ds(pl.multiple_of(source * width, width), width)],
                (((1,), (1,)), ((), ())),
                preferred_element_type=F32,
            )
            total = term if total is None else total + term
        return total

    local[6].wait()
    local[7].wait()
    near = [(dx, dy) for dx in (0, 1, 3) for dy in (0, 1, 3)]
    far = [(dx, dy) for dx in range(SIDE) for dy in range(SIDE) if dx == 2 or dy == 2]
    total_grad[...] = grad_terms(near)
    ag_relay_far()

    take_states(0, 1)

    receive("last", view=gathered.at[pl.ds(0, 5)])
    grad = total_grad[...] + grad_terms(far)
    high = grad.astype(BF16)
    low = (grad - high.astype(F32)).astype(BF16)
    gradient[...] = inner_order(high) + inner_order(low)
    signal[...] = (gradient[...] * feats[0]).astype(BF16).astype(F32)
    finish_states(0)
    start = carried_start(1)
    states(signal, -1)
    send_states(1, -1)

    carried(conv.at[0], start, 1)
    gate[...] = (feats[0] * conv[0]).astype(BF16).reshape(length, width)

    def rs_copy(key, src, dst, axis, step):
        send(key, "rs", src, dst, plane(axis, step))

    def first_axis(h):
        return 1 if h == 0 else 0

    lower, upper = pl.ds(0, quarter), pl.ds(quarter, quarter)

    def terms(blocks):
        for dx, dy in blocks:
            dest = ((x + dx) % SIDE) * SIDE + (y + dy) % SIDE
            product = jnp.dot(
                gate[...],
                weight[:, pl.ds(pl.multiple_of(dest * width, width), width)],
                preferred_element_type=F32,
            )
            for h in range(2):
                i, j = (dx, dy) if h == 0 else (dy, dx)
                own = product[h * half : (h + 1) * half]
                if j == 2:
                    send_a[h, i] = own.astype(BF16)
                elif j == 1:
                    keep1[h, 0, i] = own[:quarter]
                    send_p[h, 0, i] = own[quarter:].astype(BF16)
                elif j == 3:
                    keep1[h, 1, i] = own[quarter:]
                    send_p[h, 1, i] = own[:quarter].astype(BF16)
                else:
                    keep0[h, i] = own

    def a_copies(*indices):
        for i in indices:
            for h in range(2):
                rs_copy(("a", h, i, 0), send_a.at[h, i, lower], recv_a.at[h, 0, i], first_axis(h), 1)
                rs_copy(("a", h, i, 1), send_a.at[h, i, upper], recv_a.at[h, 1, i], first_axis(h), -1)

    def plain_copies(*indices, ways=(0, 1)):
        for i in indices:
            for h in range(2):
                for way in ways:
                    rs_copy(("pb", h, i), send_p.at[h, way, i], recv_p.at[h, way, i], first_axis(h), 1 - 2 * way)

    def sums_on_the_way(*indices):
        for i in indices:
            for h in range(2):
                for way in range(2):
                    receive("a", h, i, way)
                    send_b[h, way, i] = (keep1[h, way, i] + recv_a[h, way, i].astype(F32)).astype(BF16)
                    rs_copy(("pb", h, i), send_b.at[h, way, i], recv_b.at[h, way, i], first_axis(h), 1 - 2 * way)

    terms(((2, 2),))
    a_copies(2)
    terms(((2, 1), (1, 2)))
    plain_copies(2, ways=(0,))
    a_copies(1)
    terms(((2, 3), (3, 2)))
    plain_copies(2, ways=(1,))
    a_copies(3)
    terms(((1, 1), (1, 3), (3, 1), (3, 3)))
    sums_on_the_way(2)
    terms(((2, 0), (0, 2)))
    a_copies(0)
    plain_copies(1, 3)
    terms(((0, 1), (1, 0), (0, 3), (3, 0), (0, 0)))
    sums_on_the_way(1, 3)
    plain_copies(0)
    sums_on_the_way(0)

    def edges(s, key):
        for j in range(16):
            small[j : j + 1, :] = gfeats[s, j, 0:1, :]
        edge_send[s] = small[0:16].astype(BF16)
        send(key, key, edge_send.at[s], edge_recv.at[s], at_ctx(before))

    gfeats[0, 0:rows] = (gradient[...] * conv[0]).astype(BF16).astype(F32)
    edges(0, ("edge", 0))
    conv[1] = filt[0][None] * signal[...]
    for d in range(1, rows):
        conv[1, 0 : rows - d] = conv[1, 0 : rows - d] + filt[d][None] * signal[d:rows]

    def collect(h, i):
        receive("pb", h, i, view=send_a.at[h, pl.ds(0, 2)])
        low = keep0[h, i, 0:quarter] + recv_b[h, 0, i].astype(F32) + recv_p[h, 1, i].astype(F32)
        high = keep0[h, i, quarter:half] + recv_p[h, 0, i].astype(F32) + recv_b[h, 1, i].astype(F32)
        return low, high

    for h in range(2):
        axis = 1 - first_axis(h)
        low, high = collect(h, 2)
        part2[h, 0] = low.astype(BF16)
        part2[h, 1] = high.astype(BF16)
        rs_copy(("a2", h, 0), part2.at[h, 0], recv2_a.at[h, 0], axis, 1)
        rs_copy(("a2", h, 1), part2.at[h, 1], recv2_a.at[h, 1], axis, -1)

    last = (ctx < n_ctx - 1).astype(F32)

    def featurize_back(s):
        small[0:16] = edge_recv[s].astype(F32) * last
        for j in range(taps_len - 1):
            moved = pltpu.roll(gfeats[s, j], SUB - 1, 0)
            gfeats[s, rows + j] = jnp.where(
                place == SUB - 1, jnp.broadcast_to(small[j : j + 1, :], (SUB, width)), moved
            )
        total = jnp.zeros((rows, SUB, width), F32)
        for j in range(taps_len):
            total = total + taps[s, j : j + 1, :][None] * gfeats[s, j : j + rows]
        (gq_out, gk_out, gv_out)[s][...] = token_order(total.astype(BF16).reshape(length, width))

    take_states(1, -1)
    receive("edge", 0)
    featurize_back(0)
    finish_states(1)
    carried(conv.at[1], carried_start(-1), -1)
    gfeats[1, 0:rows] = (conv[1] * feats[2]).astype(BF16).astype(F32)
    edges(1, ("edge", 1))
    gfeats[2, 0:rows] = (conv[1] * feats[1]).astype(BF16).astype(F32)
    edges(2, ("edge", 1))

    for h in range(2):
        axis = 1 - first_axis(h)
        low, high = collect(h, 1)
        own2[h, 0] = low
        part2[h, 2] = high.astype(BF16)
        rs_copy(("pb2", h), part2.at[h, 2], recv2_p.at[h, 0], axis, 1)
        low, high = collect(h, 3)
        own2[h, 1] = high
        part2[h, 3] = low.astype(BF16)
        rs_copy(("pb2", h), part2.at[h, 3], recv2_p.at[h, 1], axis, -1)
        for way in range(2):
            receive("a2", h, way)
            send2_b[h, way] = (own2[h, way] + recv2_a[h, way].astype(F32)).astype(BF16)
            rs_copy(("pb2", h), send2_b.at[h, way], recv2_b.at[h, way], axis, 1 - 2 * way)
    for h in range(2):
        low, high = collect(h, 0)
        own2[h, 2] = low
        own2[h, 3] = high

    receive("edge", 1, view=edge_recv.at[pl.ds(0, 2)])
    featurize_back(1)
    featurize_back(2)

    for h in range(2):
        receive("pb2", h, view=send_a.at[h, pl.ds(0, 2)])
        low = own2[h, 2] + recv2_b[h, 0].astype(F32) + recv2_p[h, 1].astype(F32)
        high = own2[h, 3] + recv2_p[h, 0].astype(F32) + recv2_b[h, 1].astype(F32)
        gate[h * half : h * half + quarter] = low.astype(BF16)
        gate[h * half + quarter : (h + 1) * half] = high.astype(BF16)
    proj_out[...] = token_order(gate[...])

    views = {
        "ag": gathered.at[pl.ds(0, SIDE * SIDE - 1)],
        "rs": gathered.at[pl.ds(0, SIDE * SIDE - 1)],
        "halo": halo,
        ("z", 0): s_recv.at[0],
        ("z", 1): s_recv.at[1],
        ("x", 0): x_recv.at[0],
        ("x", 1): x_recv.at[1],
        ("edge", 0): edge_recv.at[0],
        ("edge", 1): edge_recv.at[pl.ds(0, 2)],
    }
    assert (len(sent_on), len(slots)) == (SENDS, RECEIVES)
    for group, index in sent_on.items():
        pltpu.make_async_copy(views[group], views[group], send_sem.at[index]).wait()


def deliver(*refs):
    sources, targets, sem = refs[:4], refs[4:8], refs[8]
    copies = [pltpu.make_async_copy(sources[i], targets[i], sem.at[i]) for i in range(4)]
    for copy in copies:
        copy.start()
    for copy in copies:
        copy.wait()


def shards(query_in, key_in, value_in, short_taps, residues, decays, out_weight, out_grad):
    length, width = query_in.shape
    rows = length // SUB
    half, quarter = length // 2, length // 4
    short_taps = jnp.transpose(short_taps, (1, 0, 2))
    residues, decays = residues.T, decays.T
    taps_len = short_taps.shape[1]
    modes = decays.shape[0]
    chips = lax.axis_size("ctx") // 2
    vmem = pltpu.VMEM
    dma = pltpu.SemaphoreType.DMA
    scratch = [
        vmem((3, length, width), BF16),
        vmem(short_taps.shape, F32),
        vmem(residues.shape, F32),
        vmem(decays.shape, F32),
        vmem(out_weight.shape, BF16),
        vmem((SIDE * SIDE, length, width), BF16),
        vmem((3, 16, width), BF16),
        vmem((3, rows + 8, SUB, width), F32),
        vmem((3, rows, SUB, width), F32),
        vmem((rows, SUB, width), F32),
        vmem((2, rows, SUB, width), F32),
        vmem((rows, SUB, width), F32),
        vmem((length, width), F32),
        vmem((rows, SUB, width), F32),
        vmem((rows, width), F32),
        vmem((2, modes, width), F32),
        vmem((7, modes, SUB, width), F32),
        vmem((modes, SUB, width), F32),
        vmem((modes, SUB, width), F32),
        vmem((2, modes, width), BF16),
        vmem((2, chips - 1, modes, width), BF16),
        vmem((2, modes, width), F32),
        vmem((2, modes, width), F32),
        vmem((2, modes, width), F32),
        vmem((length, width), BF16),
        vmem((2, SIDE, half, width), F32),
        vmem((2, 2, SIDE, quarter, width), F32),
        vmem((2, SIDE, half, width), BF16),
        vmem((2, 2, SIDE, quarter, width), BF16),
        vmem((2, 2, SIDE, quarter, width), BF16),
        vmem((2, 2, SIDE, quarter, width), BF16),
        vmem((2, 2, SIDE, quarter, width), BF16),
        vmem((2, 2, SIDE, quarter, width), BF16),
        vmem((2, 4, quarter, width), BF16),
        vmem((2, 4, quarter, width), F32),
        vmem((2, 2, quarter, width), BF16),
        vmem((2, 2, quarter, width), BF16),
        vmem((2, 2, quarter, width), BF16),
        vmem((2, 2, quarter, width), BF16),
        vmem((3, rows + 8, SUB, width), F32),
        vmem((3, 16, width), BF16),
        vmem((3, 16, width), BF16),
        vmem((length, length), BF16),
        vmem((length, length), BF16),
        dma((8,)),
        dma((SENDS,)),
        dma((RECEIVES,)),
        pltpu.SemaphoreType.REGULAR((2,)),
    ]
    out = jax.ShapeDtypeStruct((length, width), BF16)
    results = pl.pallas_call(
        functools.partial(kernel, chips, modes, taps_len),
        out_shape=(out, out, out, out),
        in_specs=[pl.BlockSpec(memory_space=pl.ANY)] * 8,
        out_specs=[pl.BlockSpec(memory_space=pltpu.VMEM)] * 4,
        scratch_shapes=scratch,
        compiler_params=pltpu.CompilerParams(
            collective_id=0, has_side_effects=True, vmem_limit_bytes=56 * 1024 * 1024
        ),
        name="hyena",
    )(query_in, key_in, value_in, short_taps, residues, decays, out_weight, out_grad)
    return pl.pallas_call(
        deliver,
        out_shape=(out, out, out, out),
        in_specs=[pl.BlockSpec(memory_space=pltpu.VMEM)] * 4,
        out_specs=[pl.BlockSpec(memory_space=pl.ANY)] * 4,
        scratch_shapes=[dma((4,))],
        name="deliver",
    )(*results)


def solution(mesh):
    in_specs = (
        P("ctx", "ch"),
        P("ctx", "ch"),
        P("ctx", "ch"),
        P(None, None, "ch"),
        P("ch", None),
        P("ch", None),
        P("ch", None),
        P("ctx", "ch"),
    )
    out_specs = (P("ctx", "ch"), P("ctx", "ch"), P("ctx", "ch"), P("ctx", "ch"))
    return jax.shard_map(shards, mesh=mesh, in_specs=in_specs, out_specs=out_specs, check_vma=False)
```

time: 66.3 us -> 51.7 us (0.78)
  local copies, waits for them, and re-layouts: 10.6 us -> 0 us
  Pallas kernels: 54.8 us -> 50.9 us
    unnamed x7 -> x0, local copies, waits for them, and re-layouts: 10.6 us -> none
    pallas_call x1, Pallas kernels: 54.8 us -> 49 us  [shards(): pl.pallas_call(functools.partial(kernel, chips, modes, taps_len), out_sha...]
    pallas_call x0 -> x1, Pallas kernels: none -> 1.91 us  [shards(): pl.pallas_call(deliver, out_shape=(out, out, out, out), in_specs=[pl.Bloc...]
where the time goes in v2:
time: 51.7 us; the launch traced here: 51.6 us
  Pallas kernels  50.9 us (98%)
  between operations  0.64 us (1%)
    pallas_call x1, Pallas kernels, shards(): pl.pallas_call(functools.partial(kernel, chips, modes, taps_len), out_sha...  49 us
    pallas_call x1, Pallas kernels, shards(): pl.pallas_call(deliver, out_shape=(out, out, out, out), in_specs=[pl.Bloc...  1.91 us

profile of v2, /device:TPU:1, one launch (start us, length us, event | category | flops | bytes accessed | tf_op | source)
XLA Modules:
  0.0 51.6 jit_solution(15434976486058748990)
XLA Ops:
  0.6 49.0 %hyena.1 = (bf16[256,256]{1,0:T(8,128)(2,1)}, bf16[256,256]{1,0:T(8,128)(2,1)}, bf16[256,256]{1,0:T(8,128)(2,1)}, bf16[256,256]{1,0:T(8,128)(2,1)}) custom-call(bf16[256,256]{1,0:T(8,128)(2,1)} %q_in.1, bf16[256,256]{1,0:T(8,128)(2,1)} %k_in.1, bf16[256,256]{1,0:T(8,128)(2,1)} %v_in.1, f32[3,7,256]{2,1,0:T(8,128)} %bitcast.3, f32[16,256]{1,0:T(8,128)} %bitcast.4, ...), custom_call_target="tpu_custom_call" | custom-call | tf_op jit(solution)/shard_map/hyena/pallas_call | solution.py:649
  49.7 1.9 %deliver.1 = (bf16[256,256]{1,0:T(8,128)(2,1)}, bf16[256,256]{1,0:T(8,128)(2,1)}, bf16[256,256]{1,0:T(8,128)(2,1)}, bf16[256,256]{1,0:T(8,128)(2,1)}) custom-call(bf16[256,256]{1,0:T(8,128)(2,1)} %get-tuple-element.8.refs_0_, bf16[256,256]{1,0:T(8,128)(2,1)} %get-tuple-element.9.refs_1_, bf16[256,256]{1,0:T(8,128)(2,1)} %get-tuple-element.10.refs_2_, ...), custom_call_target="tpu_custom_call" | custom-call | tf_op jit(solution)/shard_map/deliver/pallas_call | solution.py:660

commit v3 on v2

--- a/solution.py
+++ b/solution.py
@@ -12,6 +12,8 @@
 BF16 = jnp.bfloat16
 SIDE = 4
 SUB = 8
+LANES = 128
+UNROLL = 2
 SENDS, RECEIVES = 9, 62
 
 
@@ -278,11 +280,18 @@
     pass_news()
 
     def states(signal, direction):
-        def advance(r, total):
-            at = r if direction == 1 else rows - 1 - r
-            return total * decay[0] + signal[at][None]
-
-        total = lax.fori_loop(0, rows, advance, jnp.zeros((modes, SUB, width), F32))
+        for lo in range(0, width, LANES):
+            cols = slice(lo, lo + LANES)
+            step_decay = decay[0, :, :, cols]
+
+            def advance(r, total):
+                for k in range(UNROLL):
+                    at = UNROLL * r + k if direction == 1 else rows - 1 - k - UNROLL * r
+                    total = total * step_decay + signal[at, :, cols][None]
+                return total
+
+            scan_buf[:, :, cols] = lax.fori_loop(0, rows // UNROLL, advance, jnp.zeros((modes, SUB, LANES), F32))
+        total = scan_buf[...]
         for level, step in enumerate((1, 2, 4)):
             if direction == 1:
                 moved = jnp.where(sublane >= step, pltpu.roll(total, step, 1), 0.0)
@@ -334,12 +343,18 @@
         return decay[6] * decay[0] * (prefix[...] + reach * scan_buf[...])
 
     def carried(out, start, direction):
-        def advance(r, state):
-            at = r if direction == 1 else rows - 1 - r
-            out[at] = out[at] + jnp.sum(state, axis=0)
-            return state * decay[0]
-
-        lax.fori_loop(0, rows, advance, start)
+        for lo in range(0, width, LANES):
+            cols = slice(lo, lo + LANES)
+            step_decay = decay[0, :, :, cols]
+
+            def advance(r, state):
+                for k in range(UNROLL):
+                    at = UNROLL * r + k if direction == 1 else rows - 1 - k - UNROLL * r
+                    out[at, :, cols] = out[at, :, cols] + jnp.sum(state, axis=0)
+                    state = state * step_decay
+                return state
+
+            lax.fori_loop(0, rows // UNROLL, advance, start[:, :, cols])
 
     for s in range(3):
         local[s].wait()
@@ -365,14 +380,15 @@
     while news[0] < len(reaches):
         pass_news()
     send_states(0, 1)
+    ag_far()
     ag_relay2(0)
-    ag_far()
 
     conv[0] = filt[0][None] * signal[...]
     for d in range(1, rows):
         conv[0, d:rows] = conv[0, d:rows] + filt[d][None] * signal[0 : rows - d]
     ag_relay2(1)
     ag_relay2(3)
+    ag_relay_far()
 
     def grad_terms(blocks):
         total = None
@@ -392,7 +408,6 @@
     near = [(dx, dy) for dx in (0, 1, 3) for dy in (0, 1, 3)]
     far = [(dx, dy) for dx in range(SIDE) for dy in range(SIDE) if dx == 2 or dy == 2]
     total_grad[...] = grad_terms(near)
-    ag_relay_far()
 
     take_states(0, 1)
 
@@ -403,11 +418,8 @@
     gradient[...] = inner_order(high) + inner_order(low)
     signal[...] = (gradient[...] * feats[0]).astype(BF16).astype(F32)
     finish_states(0)
-    start = carried_start(1)
-    states(signal, -1)
-    send_states(1, -1)
-
-    carried(conv.at[0], start, 1)
+
+    carried(conv.at[0], carried_start(1), 1)
     gate[...] = (feats[0] * conv[0]).astype(BF16).reshape(length, width)
 
     def rs_copy(key, src, dst, axis, step):
@@ -465,18 +477,21 @@
     terms(((2, 1), (1, 2)))
     plain_copies(2, ways=(0,))
     a_copies(1)
+
+    states(signal, -1)
+    send_states(1, -1)
+
     terms(((2, 3), (3, 2)))
     plain_copies(2, ways=(1,))
     a_copies(3)
     terms(((1, 1), (1, 3), (3, 1), (3, 3)))
+    plain_copies(1, 3)
     sums_on_the_way(2)
+    sums_on_the_way(1, 3)
     terms(((2, 0), (0, 2)))
     a_copies(0)
-    plain_copies(1, 3)
     terms(((0, 1), (1, 0), (0, 3), (3, 0), (0, 0)))
-    sums_on_the_way(1, 3)
     plain_copies(0)
-    sums_on_the_way(0)
 
     def edges(s, key):
         for j in range(16):
@@ -503,6 +518,7 @@
         part2[h, 1] = high.astype(BF16)
         rs_copy(("a2", h, 0), part2.at[h, 0], recv2_a.at[h, 0], axis, 1)
         rs_copy(("a2", h, 1), part2.at[h, 1], recv2_a.at[h, 1], axis, -1)
+    sums_on_the_way(0)
 
     last = (ctx < n_ctx - 1).astype(F32)
 
@@ -519,14 +535,6 @@
         (gq_out, gk_out, gv_out)[s][...] = token_order(total.astype(BF16).reshape(length, width))
 
     take_states(1, -1)
-    receive("edge", 0)
-    featurize_back(0)
-    finish_states(1)
-    carried(conv.at[1], carried_start(-1), -1)
-    gfeats[1, 0:rows] = (conv[1] * feats[2]).astype(BF16).astype(F32)
-    edges(1, ("edge", 1))
-    gfeats[2, 0:rows] = (conv[1] * feats[1]).astype(BF16).astype(F32)
-    edges(2, ("edge", 1))
 
     for h in range(2):
         axis = 1 - first_axis(h)
@@ -542,6 +550,15 @@
             receive("a2", h, way)
             send2_b[h, way] = (own2[h, way] + recv2_a[h, way].astype(F32)).astype(BF16)
             rs_copy(("pb2", h), send2_b.at[h, way], recv2_b.at[h, way], axis, 1 - 2 * way)
+
+    finish_states(1)
+    carried(conv.at[1], carried_start(-1), -1)
+    gfeats[1, 0:rows] = (conv[1] * feats[2]).astype(BF16).astype(F32)
+    edges(1, ("edge", 1))
+    gfeats[2, 0:rows] = (conv[1] * feats[1]).astype(BF16).astype(F32)
+    edges(2, ("edge", 1))
+    receive("edge", 0)
+    featurize_back(0)
     for h in range(2):
         low, high = collect(h, 0)
         own2[h, 2] = low
@@ -648,7 +665,7 @@
     out = jax.ShapeDtypeStruct((length, width), BF16)
     results = pl.pallas_call(
         functools.partial(kernel, chips, modes, taps_len),
-        out_shape=(out, out, out, out),
+        out_shape=(pltpu.VMEM((length, width), BF16),) * 4,
         in_specs=[pl.BlockSpec(memory_space=pl.ANY)] * 8,
         out_specs=[pl.BlockSpec(memory_space=pltpu.VMEM)] * 4,
         scratch_shapes=scratch,
@@ -664,7 +681,7 @@
         out_specs=[pl.BlockSpec(memory_space=pl.ANY)] * 4,
         scratch_shapes=[dma((4,))],
         name="deliver",
-    )(*results)
+    )(*[pltpu.with_memory_space_constraint(r, pltpu.VMEM) for r in results])
 
 
 def solution(mesh):

time: 51.7 us -> 49.5 us (0.957)
  Pallas kernels: 50.9 us -> 48.7 us
    pallas_call x1, Pallas kernels: 49 us -> 47.9 us  [shards(): pl.pallas_call(functools.partial(kernel, chips, modes, taps_len), out_sha...]
    pallas_call x1, Pallas kernels: 1.91 us -> 0.82 us  [shards(): pl.pallas_call(deliver, out_shape=(out, out, out, out), in_specs=[pl.Bloc...]
where the time goes in v3:
time: 49.5 us; the launch traced here: 49.4 us
  Pallas kernels  48.7 us (98%)
  between operations  0.64 us (1%)
    pallas_call x1, Pallas kernels, shards(): pl.pallas_call(functools.partial(kernel, chips, modes, taps_len), out_sha...  47.9 us

profile of v3, /device:TPU:1, one launch (start us, length us, event | category | flops | bytes accessed | tf_op | source)
XLA Modules:
  0.0 49.4 jit_solution(11925555186791264886)
XLA Ops:
  0.6 47.9 %hyena.1 = (bf16[256,256]{1,0:T(8,128)(2,1)S(1)}, bf16[256,256]{1,0:T(8,128)(2,1)S(1)}, bf16[256,256]{1,0:T(8,128)(2,1)S(1)}, bf16[256,256]{1,0:T(8,128)(2,1)S(1)}) custom-call(bf16[256,256]{1,0:T(8,128)(2,1)} %q_in.1, bf16[256,256]{1,0:T(8,128)(2,1)} %k_in.1, bf16[256,256]{1,0:T(8,128)(2,1)} %v_in.1, f32[3,7,256]{2,1,0:T(8,128)} %bitcast.3, ...), custom_call_target="tpu_custom_call" | custom-call | tf_op jit(solution)/shard_map/hyena/pallas_call | solution.py:666
  48.6 0.8 %deliver.1 = (bf16[256,256]{1,0:T(8,128)(2,1)}, bf16[256,256]{1,0:T(8,128)(2,1)}, bf16[256,256]{1,0:T(8,128)(2,1)}, bf16[256,256]{1,0:T(8,128)(2,1)}) custom-call(bf16[256,256]{1,0:T(8,128)(2,1)S(1)} %get-tuple-element.8.refs_0_, bf16[256,256]{1,0:T(8,128)(2,1)S(1)} %get-tuple-element.9.refs_1_, bf16[256,256]{1,0:T(8,128)(2,1)S(1)} %get-tuple-element.10.refs_2_, ...), custom_call_target="tpu_custom_call" | custom-call | tf_op jit(solution)/shard_map/deliver/pallas_call | solution.py:677

commit v4 on v3

--- a/solution.py
+++ b/solution.py
@@ -411,12 +411,6 @@
 
     take_states(0, 1)
 
-    receive("last", view=gathered.at[pl.ds(0, 5)])
-    grad = total_grad[...] + grad_terms(far)
-    high = grad.astype(BF16)
-    low = (grad - high.astype(F32)).astype(BF16)
-    gradient[...] = inner_order(high) + inner_order(low)
-    signal[...] = (gradient[...] * feats[0]).astype(BF16).astype(F32)
     finish_states(0)
 
     carried(conv.at[0], carried_start(1), 1)
@@ -478,6 +472,12 @@
     plain_copies(2, ways=(0,))
     a_copies(1)
 
+    receive("last", view=gathered.at[pl.ds(0, 5)])
+    grad = total_grad[...] + grad_terms(far)
+    high = grad.astype(BF16)
+    low = (grad - high.astype(F32)).astype(BF16)
+    gradient[...] = inner_order(high) + inner_order(low)
+    signal[...] = (gradient[...] * feats[0]).astype(BF16).astype(F32)
     states(signal, -1)
     send_states(1, -1)
 

time: 49.5 us -> 47.2 us (0.954)
  Pallas kernels: 48.7 us -> 46.5 us
    pallas_call x1, Pallas kernels: 47.9 us -> 45.6 us  [shards(): pl.pallas_call(functools.partial(kernel, chips, modes, taps_len), out_sha...]
where the time goes in v4:
time: 47.2 us; the launch traced here: 47.1 us
  Pallas kernels  46.5 us (99%)
  between operations  0.64 us (1%)
    pallas_call x1, Pallas kernels, shards(): pl.pallas_call(functools.partial(kernel, chips, modes, taps_len), out_sha...  45.6 us

profile of v4, /device:TPU:1, one launch (start us, length us, event | category | flops | bytes accessed | tf_op | source)
XLA Modules:
  0.0 47.1 jit_solution(16996031928478394381)
XLA Ops:
  0.6 45.6 %hyena.1 = (bf16[256,256]{1,0:T(8,128)(2,1)S(1)}, bf16[256,256]{1,0:T(8,128)(2,1)S(1)}, bf16[256,256]{1,0:T(8,128)(2,1)S(1)}, bf16[256,256]{1,0:T(8,128)(2,1)S(1)}) custom-call(bf16[256,256]{1,0:T(8,128)(2,1)} %q_in.1, bf16[256,256]{1,0:T(8,128)(2,1)} %k_in.1, bf16[256,256]{1,0:T(8,128)(2,1)} %v_in.1, f32[3,7,256]{2,1,0:T(8,128)} %bitcast.3, ...), custom_call_target="tpu_custom_call" | custom-call | tf_op jit(solution)/shard_map/hyena/pallas_call | solution.py:666
  46.3 0.8 %deliver.1 = (bf16[256,256]{1,0:T(8,128)(2,1)}, bf16[256,256]{1,0:T(8,128)(2,1)}, bf16[256,256]{1,0:T(8,128)(2,1)}, bf16[256,256]{1,0:T(8,128)(2,1)}) custom-call(bf16[256,256]{1,0:T(8,128)(2,1)S(1)} %get-tuple-element.8.refs_0_, bf16[256,256]{1,0:T(8,128)(2,1)S(1)} %get-tuple-element.9.refs_1_, bf16[256,256]{1,0:T(8,128)(2,1)S(1)} %get-tuple-element.10.refs_2_, ...), custom_call_target="tpu_custom_call" | custom-call | tf_op jit(solution)/shard_map/deliver/pallas_call | solution.py:677
